TPU v7x, 256 devices: a whole 4x4x8 slice. The times are simulated.
256 devices in a mesh: row: 32 (over z, x_lo, core), col: 8 (over x_hi, y).
Axes of the slice: x: 4 (x_hi: 2, x_lo: 2; x = x_hi * 2 + x_lo), y: 4, z: 8, core: 2. Of those that a mesh axis runs over, the one named last changes fastest.
Arguments:
- polar_rays: bfloat16 [256, 360, 256], P(('row', 'col')), may hold values from -6 to 6
- first_line: int32 [256, 32, 8], P('row', None, 'col'), may hold values from 0 to 359
- second_line: int32 [256, 32, 8], P('row', None, 'col'), may hold values from 0 to 179
- start_frame: float32 [3, 3, 256], P(None, None, ('row', 'col')), may hold values from -6 to 6
Outputs:
- line_scores: float32 [256, 32, 8], P('row', None, 'col')
- estimates: float32 [3, 3, 256], P(None, None, ('row', 'col'))
All inputs are finite; a program needn't handle non-finite values. Where the computation divides by a largest or mean magnitude, that divisor is 1e-20 or more.
Results may differ from a plain program's by a relative error of at most 0.0003.
Values may be sent and summed in bfloat16 or wider, within the bound.
A program may use at most 64 MiB of HBM per device.

v0:
```python
import math

import jax
import jax.numpy as jnp
from jax import lax
from jax.sharding import PartitionSpec as P

L = 360
ITERS = 3


def unit_vectors(angle):
    phases = angle.astype(jnp.float32) * (2.0 * math.pi / L)
    return jnp.stack([jnp.cos(phases), jnp.sin(phases), jnp.ones_like(phases)])


def lower_solve(factor, values):
    first_row = values[0] / factor[0, 0]
    second_row = (values[1] - factor[1, 0] * first_row) / factor[1, 1]
    third_row = (values[2] - factor[2, 0] * first_row - factor[2, 1] * second_row) / factor[2, 2]
    return jnp.stack([first_row, second_row, third_row])


def per_device(polar_rays, first_line, second_line, start_frame):
    blocks = polar_rays.shape[0]
    exact = lax.Precision.HIGHEST
    row_rays = lax.all_gather(polar_rays, "col", axis=0, tiled=True)
    row_count = row_rays.shape[0]
    first_all = first_line.reshape(row_count, -1)
    second_all = second_line.reshape(row_count, -1)
    half_rays = polar_rays[:, : L // 2]
    block_rays = lax.all_gather(half_rays, "row", axis=0, tiled=True)

    def score_row(inputs):
        own_rays, first_row, second_row = inputs
        corr = jnp.einsum("ar,jbr->jab", own_rays, block_rays, preferred_element_type=jnp.float32)
        center = corr - jnp.mean(corr, axis=(1, 2), keepdims=True)
        spread = jnp.mean(jnp.abs(center), axis=(1, 2))
        picked = jnp.take_along_axis(center, first_row[:, None, None], axis=1)[:, 0, :]
        picked = jnp.take_along_axis(picked, second_row[:, None], axis=1)[:, 0]
        return picked / (spread + 1e-05)

    scores = lax.map(score_row, (row_rays, first_all, second_all))
    first_units = unit_vectors(first_all)
    second_weighted = scores[None] * unit_vectors(second_all)
    frames = start_frame
    for turn_index in range(ITERS):
        col_frames = lax.all_gather(frames, "row", axis=2, tiled=True)
        mixed = jnp.einsum("qij,kqj->kij", second_weighted, col_frames, precision=exact)
        applied = jnp.einsum("pij,kij->kpi", first_units, mixed, precision=exact)
        row_total = lax.psum(applied, "col")
        gram_part = jnp.einsum("kpi,lpi->kl", row_total, row_total, precision=exact)
        gram_matrix = lax.psum(gram_part, "row")
        own_part = lax.dynamic_slice_in_dim(row_total, lax.axis_index("col") * blocks, blocks, 2)
        factor = jnp.linalg.cholesky(gram_matrix)
        frames = lower_solve(factor, own_part)
    image_count = blocks * lax.axis_size("row") * lax.axis_size("col")
    return (scores.reshape(first_line.shape), math.sqrt(image_count) * frames)


def solution(mesh):
    placed = (
        P(("row", "col"), None, None),
        P("row", None, "col"),
        P("row", None, "col"),
        P(None, None, ("row", "col")),
    )
    return jax.shard_map(
        per_device,
        mesh=mesh,
        in_specs=placed,
        out_specs=(P("row", None, "col"), P(None, None, ("row", "col"))),
        check_vma=False,
    )
```

profile of v0, /device:TPU:1, one launch (start us, length us, event | category | flops | bytes accessed | tf_op | source)
XLA Modules:
  0.0 690.3 jit_solution(8122326232665140078)
XLA Ops:
  7.9 1.5 slice.88
  10.3 38.6 %all_gather.17 = f32[3,3,32]{1,0,2:T(4,128)S(1)} all-gather(f32[3,3,1]{1,0,2:T(4,128)S(1)} %copy.72), channel_id=1, replica_groups=mesh['row'=32,'col'=8] {'row'}, dimensions={2}, use_global_device_ids=true | all-gather | bytes 1188 | tf_op jit(solution)/shard_map/all_gather | solution.py:48
  49.6 18.2 %all-gather.3.cloned.1.call-done = bf16[8,360,256]{2,1,0:T(8,128)(2,1)} async-done(((bf16[1,360,256]{2,1,0:T(8,128)(2,1)}), bf16[8,360,256]{2,1,0:T(8,128)(2,1)}) %all-gather.3.cloned.1.call-update) | async-done | bytes 1474576 | tf_op jit(solution)/shard_map/all_gather | solution.py:27
  67.8 67.8 %all-gather.5.cloned.1.call-done = bf16[32,180,256]{2,1,0:T(8,128)(2,1)} async-done(((bf16[1,180,256]{2,1,0:T(8,128)(2,1)}), bf16[32,180,256]{2,1,0:T(8,128)(2,1)}) %all-gather.5.cloned.1.call-update) | async-done | bytes 2949136 | tf_op jit(solution)/shard_map/all_gather | solution.py:32
  135.6 191.5 %while.10 = (s32[]{:T(128)}, f32[8,32]{1,0:T(8,128)S(1)}, s32[8,32]{1,0:T(8,128)}, s32[8,32]{1,0:T(8,128)}, bf16[8,360,256]{2,1,0:T(8,128)(2,1)}, /*index=5*/bf16[32,180,256]{2,1,0:T(8,128)(2,1)}, s32[]{:T(128)}, s32[]{:T(128)}) while((s32[]{:T(128)}, f32[8,32]{1,0:T(8,128)S(1)}, s32[8,32]{1,0:T(8,128)}, s32[8,32]{1,0:T(8,128)}, ...), condition=%wide.region_3.4_spmd, body=%wide.region_0.3_spmd.sunk | while | flops 1069984576 | bytes 44767920 | solution.py:43
  135.6 3.8 fusion.39
  139.4 4.5 abs_reduce_fusion.2
  143.9 11.2 %copy.109 = f32[32,360,180]{2,1,0:T(8,128)} copy(f32[32,360,180]{1,2,0:T(8,128)} %get-tuple-element.146) | data formatting | bytes 16588800 | tf_op jit(solution)/shard_map/while/body/eval_jaxpr/sub | solution.py:37
  155.8 1.4 gather_fusion
  159.5 3.8 fusion.39
  163.3 4.5 abs_reduce_fusion.2
  167.8 11.2 %copy.109 = f32[32,360,180]{2,1,0:T(8,128)} copy(f32[32,360,180]{1,2,0:T(8,128)} %get-tuple-element.146) | data formatting | bytes 16588800 | tf_op jit(solution)/shard_map/while/body/eval_jaxpr/sub | solution.py:37
  179.8 1.4 gather_fusion
  183.4 3.8 fusion.39
  187.3 4.5 abs_reduce_fusion.2
  191.8 11.2 %copy.109 = f32[32,360,180]{2,1,0:T(8,128)} copy(f32[32,360,180]{1,2,0:T(8,128)} %get-tuple-element.146) | data formatting | bytes 16588800 | tf_op jit(solution)/shard_map/while/body/eval_jaxpr/sub | solution.py:37
  203.7 1.4 gather_fusion
  207.4 3.8 fusion.39
  211.2 4.5 abs_reduce_fusion.2
  215.7 11.2 %copy.109 = f32[32,360,180]{2,1,0:T(8,128)} copy(f32[32,360,180]{1,2,0:T(8,128)} %get-tuple-element.146) | data formatting | bytes 16588800 | tf_op jit(solution)/shard_map/while/body/eval_jaxpr/sub | solution.py:37
  227.6 1.4 gather_fusion
  231.3 3.8 fusion.39
  235.1 4.5 abs_reduce_fusion.2
  239.6 11.2 %copy.109 = f32[32,360,180]{2,1,0:T(8,128)} copy(f32[32,360,180]{1,2,0:T(8,128)} %get-tuple-element.146) | data formatting | bytes 16588800 | tf_op jit(solution)/shard_map/while/body/eval_jaxpr/sub | solution.py:37
  251.6 1.4 gather_fusion
  255.2 3.8 fusion.39
  259.1 4.5 abs_reduce_fusion.2
  263.6 11.2 %copy.109 = f32[32,360,180]{2,1,0:T(8,128)} copy(f32[32,360,180]{1,2,0:T(8,128)} %get-tuple-element.146) | data formatting | bytes 16588800 | tf_op jit(solution)/shard_map/while/body/eval_jaxpr/sub | solution.py:37
  275.5 1.4 gather_fusion
  279.2 3.8 fusion.39
  283.0 4.5 abs_reduce_fusion.2
  287.5 11.2 %copy.109 = f32[32,360,180]{2,1,0:T(8,128)} copy(f32[32,360,180]{1,2,0:T(8,128)} %get-tuple-element.146) | data formatting | bytes 16588800 | tf_op jit(solution)/shard_map/while/body/eval_jaxpr/sub | solution.py:37
  299.4 1.4 gather_fusion
  303.1 3.8 fusion.39
  306.9 4.5 abs_reduce_fusion.2
  311.4 11.2 %copy.109 = f32[32,360,180]{2,1,0:T(8,128)} copy(f32[32,360,180]{1,2,0:T(8,128)} %get-tuple-element.146) | data formatting | bytes 16588800 | tf_op jit(solution)/shard_map/while/body/eval_jaxpr/sub | solution.py:37
  323.4 1.4 gather_fusion
  327.8 34.2 %psum.42 = f32[3,3,8]{1,0,2:T(4,128)S(1)} all-reduce(f32[3,3,8]{1,0,2:T(4,128)S(1)} %convolution_bitcast_fusion.4), channel_id=1, replica_groups=mesh['row'=32,'col'=8] {'col'}, use_global_device_ids=true, to_apply=%region_4.5 | all-reduce | flops 72 | bytes 576 | tf_op jit(solution)/shard_map/psum | solution.py:51
  362.3 59.9 %psum.43 = f32[3,3]{0,1:T(4,128)S(1)} all-reduce(f32[3,3]{0,1:T(4,128)S(1)} %convolution_bitcast_fusion.7), channel_id=1, replica_groups=mesh['row'=32,'col'=8] {'row'}, use_global_device_ids=true, to_apply=%region_5.6 | all-reduce | flops 9 | bytes 72 | tf_op jit(solution)/shard_map/psum | solution.py:53
  424.6 3.8 subtract_divide_fusion.4
  428.4 31.0 %all_gather.18 = f32[3,3,32]{1,0,2:T(4,128)S(1)} all-gather(f32[3,3,1]{1,0,2:T(4,128)S(1)} %pad_maximum_fusion), channel_id=1, replica_groups=mesh['row'=32,'col'=8] {'row'}, dimensions={2}, use_global_device_ids=true | all-gather | bytes 1188 | tf_op jit(solution)/shard_map/all_gather | solution.py:48
  460.1 29.7 %psum.44 = f32[3,3,8]{1,0,2:T(4,128)S(1)} all-reduce(f32[3,3,8]{1,0,2:T(4,128)S(1)} %convolution_bitcast_fusion.3), channel_id=1, replica_groups=mesh['row'=32,'col'=8] {'col'}, use_global_device_ids=true, to_apply=%region_8.10 | all-reduce | flops 72 | bytes 576 | tf_op jit(solution)/shard_map/psum | solution.py:51
  490.0 59.5 %psum.45 = f32[3,3]{0,1:T(4,128)S(1)} all-reduce(f32[3,3]{0,1:T(4,128)S(1)} %convolution_bitcast_fusion.6), channel_id=1, replica_groups=mesh['row'=32,'col'=8] {'row'}, use_global_device_ids=true, to_apply=%region_9.11 | all-reduce | flops 9 | bytes 72 | tf_op jit(solution)/shard_map/psum | solution.py:53
  551.9 3.8 subtract_divide_fusion.2
  555.7 31.0 %all_gather.19 = f32[3,3,32]{1,0,2:T(4,128)S(1)} all-gather(f32[3,3,1]{1,0,2:T(4,128)S(1)} %pad_maximum_fusion.1), channel_id=1, replica_groups=mesh['row'=32,'col'=8] {'row'}, dimensions={2}, use_global_device_ids=true | all-gather | bytes 1188 | tf_op jit(solution)/shard_map/all_gather | solution.py:48
  587.3 29.7 %psum.46 = f32[3,3,8]{1,0,2:T(4,128)S(1)} all-reduce(f32[3,3,8]{1,0,2:T(4,128)S(1)} %convolution_bitcast_fusion.2), channel_id=1, replica_groups=mesh['row'=32,'col'=8] {'col'}, use_global_device_ids=true, to_apply=%region_10.12 | all-reduce | flops 72 | bytes 576 | tf_op jit(solution)/shard_map/psum | solution.py:51
  617.3 59.5 %psum.47 = f32[3,3]{0,1:T(4,128)S(1)} all-reduce(f32[3,3]{0,1:T(4,128)S(1)} %convolution_bitcast_fusion.5), channel_id=1, replica_groups=mesh['row'=32,'col'=8] {'row'}, use_global_device_ids=true, to_apply=%region_11.13 | all-reduce | flops 9 | bytes 72 | tf_op jit(solution)/shard_map/psum | solution.py:53
  679.1 3.8 subtract_divide_fusion
  (143 shorter events, 36.8 us)
Async XLA Ops:
  7.2 60.6 %all-gather.3.cloned.1.call-start = ((), (), s32[]{:S(2)}) async-start(), calls=%async_computation | async-start | bytes 1658880 | tf_op jit(solution)/shard_map/all_gather | solution.py:27
  7.9 127.7 %all-gather.5.cloned.1.call-start = ((), (), s32[]{:S(2)}) async-start(), calls=%async_computation.1 | async-start | bytes 3108864 | tf_op jit(solution)/shard_map/all_gather | solution.py:32
  327.0 356.5 %copy-start = (f32[8,32]{1,0:T(8,128)}, f32[8,32]{1,0:T(8,128)S(1)}, u32[]{:S(2)}) copy-start(f32[8,32]{1,0:T(8,128)S(1)} %get-tuple-element.35) | copy-start | bytes 3076
Sparse Core Ops, SparseCore 0:
  10.6 57.1 all-gather.2
  69.6 65.8 all-gather.4
where the time goes:
time: 694 us; the launch traced here: 690 us
  blocking collectives  373 us (54%)
  local copies, waits for them, and re-layouts  113 us (16%)
  waiting for transfers between devices  86.6 us (12%)
  other arithmetic  70.8 us (10%)
  matrix products  32.8 us (5%)
  between operations  14.2 us (2%)
    psum x3, blocking collectives, per_device(): gram_matrix = lax.psum(gram_part, 'row')  179 us
    all_gather x3, blocking collectives, per_device(): col_frames = lax.all_gather(frames, 'row', axis=2, tiled=True)  101 us
    psum x3, blocking collectives, per_device(): row_total = lax.psum(applied, 'col')  93.6 us
    sub x8, local copies, waits for them, and re-layouts, score_row(): center = corr - jnp.mean(corr, axis=(1, 2), keepdims=True)  89.5 us
    all_gather x1, waiting for transfers between devices, per_device(): block_rays = lax.all_gather(half_rays, 'row', axis=0, tiled=True)  67.8 us
    reduce_sum x8, other arithmetic, score_row(): spread = jnp.mean(jnp.abs(center), axis=(1, 2))  36 us
    dot_general x8, matrix products, score_row(): jnp.einsum('ar,jbr->jab', own_rays, block_rays, preferred_element_type=jn...  30.7 us
    all_gather x1, waiting for transfers between devices, per_device(): row_rays = lax.all_gather(polar_rays, 'col', axis=0, tiled=True)  18.2 us
  transfers between devices with their start and end apart: 2, of which 2 were waited for; matrix products, arithmetic and copies ran while one was open for 0% of the time, Pallas kernels for 0%

commit v1 on v0

v1 whole, which is shorter than its diff:
```python
import functools
import math

import jax
import jax.numpy as jnp
from jax import lax
from jax.experimental import pallas as pl
from jax.experimental.pallas import tpu as pltpu
from jax.sharding import PartitionSpec as P

L = 360
HALF = 180
ITERS = 3
N = 256
PITCH = 192
SENT = 184
CUT = 176
GROUP = 4 * PITCH
TILE = 256
F32 = jnp.float32
BF16 = jnp.bfloat16
MESH = pl.DeviceIdType.MESH
HIGHEST = lax.Precision.HIGHEST


def iota(shape, dim):
    return lax.broadcasted_iota(jnp.int32, shape, dim)


def split3(x):
    hi = x.astype(BF16)
    rest = x - hi.astype(F32)
    mid = rest.astype(BF16)
    low = (rest - mid.astype(F32)).astype(BF16)
    return hi, mid, low


def permute(x, perm):
    parts = jnp.concatenate(split3(x), axis=0)
    out = jnp.dot(parts, perm, preferred_element_type=F32)
    return out[0:32] + out[32:64] + out[64:96]


def kernel(
    rays, first_ref, second_ref, second_sm, frame_ref,
    scores_ref, est_ref,
    img, grp, sel, sum_i, sum_j, first_t, acc_s, acc_m, acc_p,
    pkt, pk, own_sc, sg, yz, perm_ref, trig, hmat,
    send_sem, img_sem, grp_sem, loc_sem, many_send, many_recv,
):
    row = lax.axis_index("row")
    col = lax.axis_index("col")
    z, t, co = row // 4, (row // 2) % 2, row % 2
    xh, y = col // 4, col % 4
    rl = row % 4
    pid = rl * 8 + col
    rr = (rl, (1 - t) * 2 + co, t * 2 + 1 - co, (1 - t) * 2 + 1 - co)

    core_peer = (z * 4 + t * 2 + 1 - co, col)
    xlo_peer = (z * 4 + (1 - t) * 2 + co, col)
    zp = (((z + 1) % 8) * 4 + rl, col)
    zm = (((z + 7) % 8) * 4 + rl, col)
    xhi_peer = (row, (1 - xh) * 4 + y)
    yp = (row, xh * 4 + (y + 1) % 4)
    ym = (row, xh * 4 + (y + 3) % 4)

    own_img = pltpu.make_async_copy(rays.at[0], img.at[0], loc_sem.at[0])
    own_img.start()

    def plane_peer(d):
        peer = (pid + d) % 32
        return (z * 4 + peer // 8, peer % 8)

    def z_peer(d):
        return (((z + d) % 8) * 4 + rl, col)

    barrier = pltpu.get_barrier_semaphore()

    def greet_plane(d, _):
        pl.semaphore_signal(barrier, inc=1, device_id=plane_peer(d), device_id_type=MESH)
        return 0

    def greet_z(d, _):
        pl.semaphore_signal(barrier, inc=1, device_id=z_peer(d), device_id_type=MESH)
        return 0

    lax.fori_loop(1, 32, greet_plane, 0)
    lax.fori_loop(1, 8, greet_z, 0)
    own_img.wait()

    def half(slot, block):
        return grp.at[slot, pl.ds(pl.multiple_of(block * PITCH, PITCH), SENT), :]

    own_half = pltpu.make_async_copy(img.at[0, pl.ds(0, SENT), :], half(0, rl), loc_sem.at[1])
    own_half.start()

    lane = iota((8, 128), 1)
    pkt[...] = jnp.zeros((2, 8, 128), F32)
    pkt[0, 0:8, 0:32] = (first_ref[...] + 512 * second_ref[...]).astype(F32)
    pkt[1, 0:3, 0:3] = frame_ref[...]
    packed = pkt[0]
    frame = pkt[1]
    for q in range(3):
        packed = packed + jnp.where(lane == 32 + q * 32 + pid, frame[:, q : q + 1], 0.0)
    pkt[0] = packed
    pk[pid] = packed
    own_half.wait()
    pl.semaphore_wait(barrier, 38)

    pending = []

    def send(src, dst, sem, dev):
        copy = pltpu.make_async_remote_copy(
            src_ref=src, dst_ref=dst, send_sem=send_sem.at[len(pending)], recv_sem=sem,
            device_id=dev, device_id_type=MESH,
        )
        copy.start()
        pending.append(copy)

    def landed(dst, sem):
        pltpu.make_async_remote_copy(
            src_ref=dst, dst_ref=dst, send_sem=send_sem.at[0], recv_sem=sem,
            device_id=core_peer, device_id_type=MESH,
        ).wait_recv()

    def send_half(slot, k, to_slot, to_k, dev):
        send(half(slot, rr[k]), half(to_slot, rr[k]), grp_sem.at[to_slot * 4 + to_k], dev)

    def half_landed(slot, k):
        landed(half(slot, rr[k]), grp_sem.at[slot * 4 + k])

    def whole(slot):
        return img.at[slot]

    def top(slot):
        return img.at[slot, pl.ds(0, CUT), :]

    def bottom(slot):
        return img.at[slot, pl.ds(CUT, L - CUT), :]

    send_half(0, 0, 0, 1, xlo_peer)
    send_half(0, 0, 2, 0, zp)
    send_half(0, 0, 1, 0, zm)
    send_half(0, 0, 0, 2, core_peer)
    send(whole(0), whole(4), img_sem.at[4], xhi_peer)
    send(whole(0), whole(2), img_sem.at[2], yp)
    send(whole(0), whole(1), img_sem.at[1], ym)

    def send_all(src, dst, count, peer_of, n):
        def one(d, _):
            pltpu.make_async_remote_copy(
                src_ref=src, dst_ref=dst, send_sem=many_send.at[n], recv_sem=many_recv.at[n],
                device_id=peer_of(d), device_id_type=MESH,
            ).start()
            return 0

        lax.fori_loop(1, count, one, 0)

    def all_landed(buf, count, n):
        part = buf.at[pl.ds(0, count - 1)]
        pltpu.make_async_remote_copy(
            src_ref=part, dst_ref=part, send_sem=many_send.at[n], recv_sem=many_recv.at[n],
            device_id=core_peer, device_id_type=MESH,
        ).wait()

    send_all(pkt.at[0], pk.at[pid], 32, plane_peer, 0)

    pr, pc = iota((N, N), 0), iota((N, N), 1)
    perm = jnp.where((pr // 32 == pc % 8) & (pr % 32 == pc // 8), 1.0, 0.0).astype(BF16)
    perm_ref[...] = perm
    padded = jnp.where(lane < 32, packed, 0.0).astype(jnp.int32)
    first_t[...] = jnp.transpose((padded % 512).astype(F32))
    acc_s[...] = jnp.zeros((8, 128), F32)
    acc_m[...] = jnp.zeros((8, 128), F32)
    acc_p[...] = jnp.zeros((8, 128), F32)

    def image_of(slot):
        k = slot % 4
        dy = k + (k // 2) * (5 - 2 * k)
        return ((xh + slot // 4) % 2) * 4 + (y + dy) % 4

    def plane_of(slot):
        return (z + ((slot + 1) // 2) * (2 * (slot % 2) - 1) + 8) % 8

    lanes_t = iota((32, 128), 1)

    def prep_image(slot, _):
        which = image_of(slot)
        ray = jnp.sum(jnp.where(lanes_t == which, jnp.pad(first_t[0:32, :], ((0, 0), (0, 120))), 0.0), axis=1, keepdims=True)
        data = img[slot]
        hot = jnp.where(iota((32, L), 1).astype(F32) == ray, 1.0, 0.0).astype(BF16)
        sel[slot] = jnp.dot(hot, data, preferred_element_type=F32).astype(BF16)
        total = jnp.sum(data.astype(F32).reshape(L // 8, 8, 256), axis=0)
        sum_i[slot] = jnp.broadcast_to(jnp.sum(total, axis=0, keepdims=True), (8, 256))
        return 0

    def prep_group(slot, _):
        for k in range(4):
            data = grp[slot, k * PITCH : k * PITCH + HALF, :].astype(F32)
            sum_j[slot, k : k + 1, :] = jnp.sum(data, axis=0, keepdims=True)
        return 0

    cols = iota((1, GROUP), 1)
    seg = cols // PITCH
    inside = cols % PITCH < HALF

    def unit(i, s):
        which, plane = image_of(i), plane_of(s)
        means = jnp.sum(sum_j[s] * sum_i[i], axis=1, keepdims=True) * (1.0 / (L * HALF))
        m_row = jnp.zeros((1, GROUP), F32)
        target = jnp.zeros((1, GROUP), jnp.int32)
        for k in range(4):
            m_row = jnp.where(seg == k, means[k : k + 1, :], m_row)
            target = jnp.where(seg == k, k * PITCH + second_sm[which, plane * 4 + k], target)
        lhs = jnp.concatenate([sel[i, pl.ds(pl.multiple_of((plane // 4) * 16, 16), 16), :], img[i]], axis=0)
        hit_row = (plane % 4) * 4 + seg
        found = []
        for c in range(0, GROUP, TILE):
            d = lax.dot_general(lhs, grp[s, c : c + TILE, :], (((1,), (1,)), ((), ())), preferred_element_type=F32)
            dev = jnp.sum(jnp.abs(d[16:] - m_row[:, c : c + TILE]).reshape(L // 8, 8, TILE), axis=0)
            hit = (cols[:, c : c + TILE] == target[:, c : c + TILE]) & (iota((16, TILE), 0) == hit_row[:, c : c + TILE])
            pick = jnp.where(hit, d[:16], 0.0)
            found.append(jnp.concatenate([dev, pick[0:8] + pick[8:16]], axis=0))
        both = jnp.concatenate(found, axis=1)
        here_i = iota((8, 128), 0) == which
        res_s, res_m, res_p = acc_s[...], acc_m[...], acc_p[...]
        for k in range(4):
            part = jnp.sum(jnp.where((seg == k) & inside, both, 0.0), axis=1, keepdims=True)
            here = here_i & (lane == plane * 4 + k)
            res_s = jnp.where(here, jnp.sum(part[0:8], axis=0, keepdims=True), res_s)
            res_p = jnp.where(here, jnp.sum(part[8:16], axis=0, keepdims=True), res_p)
            res_m = jnp.where(here, means[k : k + 1, :], res_m)
        acc_s[...], acc_m[...], acc_p[...] = res_s, res_m, res_p

    def block(i0, i1, s0, s1):
        def body(s, _):
            for i in range(i0, i1):
                unit(i, s)
            return 0

        lax.fori_loop(s0, s1, body, 0)

    half_landed(0, 1)
    send_half(0, 1, 2, 1, zp)
    send_half(0, 1, 1, 1, zm)
    send_half(0, 1, 0, 3, core_peer)
    lax.fori_loop(0, 1, prep_image, 0)

    def hop(to_slot, from_p, from_m, k):
        half_landed(from_p, k)
        if to_slot is not None:
            send_half(from_p, k, to_slot, k, zm)
        send_half(from_p, k, from_p, k + 2, core_peer)
        half_landed(from_m, k)
        if to_slot is not None:
            send_half(from_m, k, to_slot + 1, k, zp)
        send_half(from_m, k, from_m, k + 2, core_peer)

    hop(3, 1, 2, 0)
    half_landed(0, 2)
    half_landed(0, 3)
    landed(whole(1), img_sem.at[1])
    send(bottom(1), bottom(3), img_sem.at[3], ym)
    landed(whole(2), img_sem.at[2])
    send(top(2), top(3), img_sem.at[8], yp)
    hop(3, 1, 2, 1)
    lax.fori_loop(1, 3, prep_image, 0)
    landed(whole(4), img_sem.at[4])
    send(whole(4), whole(6), img_sem.at[6], yp)
    send(whole(4), whole(5), img_sem.at[5], ym)
    for slot in (1, 2):
        for k in (2, 3):
            half_landed(slot, k)
    lax.fori_loop(0, 3, prep_group, 0)
    block(0, 3, 0, 3)

    hop(5, 3, 4, 0)
    landed(bottom(3), img_sem.at[3])
    landed(top(3), img_sem.at[8])
    lax.fori_loop(3, 5, prep_image, 0)
    block(3, 5, 0, 3)
    hop(5, 3, 4, 1)
    for slot in (3, 4):
        for k in (2, 3):
            half_landed(slot, k)
    lax.fori_loop(3, 5, prep_group, 0)
    landed(whole(5), img_sem.at[5])
    send(bottom(5), bottom(7), img_sem.at[7], ym)
    landed(whole(6), img_sem.at[6])
    send(top(6), top(7), img_sem.at[9], yp)
    block(0, 5, 3, 5)

    half_landed(5, 0)
    send_half(5, 0, 5, 2, core_peer)
    half_landed(6, 0)
    send_half(6, 0, 7, 0, zp)
    send_half(6, 0, 6, 2, core_peer)
    half_landed(5, 1)
    send_half(5, 1, 7, 1, zm)
    send_half(5, 1, 5, 3, core_peer)
    half_landed(6, 1)
    send_half(6, 1, 6, 3, core_peer)
    landed(bottom(7), img_sem.at[7])
    landed(top(7), img_sem.at[9])
    lax.fori_loop(5, 8, prep_image, 0)
    block(5, 8, 0, 5)
    for slot in (5, 6):
        for k in (2, 3):
            half_landed(slot, k)
    half_landed(7, 0)
    send_half(7, 0, 7, 2, core_peer)
    half_landed(7, 1)
    send_half(7, 1, 7, 3, core_peer)

    all_landed(pk, 32, 0)

    def plane_tables(buf, shift):
        rows = []
        for r in range(4):
            tiles = []
            for h in range(2):
                tile = jnp.zeros((8, 128), F32)
                for c in range(4):
                    part = buf[r * 8 + h * 4 + c]
                    if shift:
                        part = jnp.where(lane < 32, part, 0.0)
                        part = pltpu.roll(part, 32 * c, 1) if c else part
                    tile = tile + part
                tiles.append(tile)
            rows.append(jnp.concatenate(tiles, axis=1))
        return jnp.concatenate(rows, axis=0)

    table = permute(plane_tables(pk, True), perm_ref[...]).astype(jnp.int32)
    angle_a = (table % 512).astype(F32) * (2.0 * math.pi / L)
    angle_b = (table // 512).astype(F32) * (2.0 * math.pi / L)
    one = jnp.ones((32, N), F32)
    unit_a = (jnp.cos(angle_a), jnp.sin(angle_a), one)
    unit_b = (jnp.cos(angle_b), jnp.sin(angle_b), one)
    for p in range(3):
        for q in range(3):
            trig[p * 32 : p * 32 + 32, q * N : q * N + N] = unit_a[p] * unit_b[q]
    frames = pk[0]
    for d in range(1, 32):
        frames = frames + pk[d]
    frames = jnp.where(lane < 96, pltpu.roll(frames, 96, 1), 0.0)
    yz[0, z] = frames
    send_all(yz.at[0, z], yz.at[0, z], 8, z_peer, 1)

    lax.fori_loop(5, 7, prep_group, 0)
    block(0, 8, 5, 7)
    half_landed(7, 2)
    half_landed(7, 3)
    lax.fori_loop(7, 8, prep_group, 0)
    block(0, 8, 7, 8)

    spread = acc_s[...] * (1.0 / (L * HALF))
    scores = (acc_p[...] - acc_m[...]) / (spread + 1e-05)
    scores = jnp.where(lane < 32, scores, 0.0)
    scores_ref[...] = scores[:, 0:32]
    wide = scores + pltpu.roll(scores, 32, 1) + pltpu.roll(scores, 64, 1) + pltpu.roll(scores, 96, 1)
    wide = jnp.where(lane // 32 == col % 4, wide, 0.0)
    own_sc[...] = wide
    sg[pid] = wide
    send_all(own_sc, sg.at[pid], 32, plane_peer, 2)
    all_landed(yz.at[0], 8, 1)
    all_landed(sg, 32, 2)
    table_s = permute(plane_tables(sg, False), perm_ref[...])
    hmat[96:128, :] = jnp.zeros((32, 3 * N), F32)
    for p in range(3):
        for q in range(3):
            at = (slice(p * 32, p * 32 + 32), slice(q * N, q * N + N))
            hmat[at] = trig[at] * table_s

    def gathered(n):
        tiles = []
        for q in range(3):
            for h in range(2):
                tile = jnp.zeros((8, 128), F32)
                for k in range(4):
                    part = yz[n, h * 4 + k]
                    shift = ((k - q) * 32) % 128
                    part = pltpu.roll(part, shift, 1) if shift else part
                    tile = jnp.where(lane // 32 == k, part, tile)
                tiles.append(tile)
        return jnp.concatenate(tiles, axis=1)

    def orthonormal(v):
        g = [jnp.sum(v * v[k : k + 1, :], axis=1, keepdims=True) for k in range(3)]
        f00 = jnp.sqrt(g[0][0:1])
        f10 = g[0][1:2] / f00
        f20 = g[0][2:3] / f00
        f11 = jnp.sqrt(g[1][1:2] - f10 * f10)
        f21 = (g[1][2:3] - f20 * f10) / f11
        f22 = jnp.sqrt(g[2][2:3] - f20 * f20 - f21 * f21)
        v0 = v[0:1] / f00
        v1 = (v[1:2] - f10 * v0) / f11
        v2 = (v[2:3] - f20 * v0 - f21 * v1) / f22
        return jnp.concatenate([v0, v1, v2, jnp.zeros((5, 3 * N), F32)], axis=0)

    v = gathered(0)
    for n in range(1, ITERS + 1):
        out = lax.dot_general(v, hmat[...], (((1,), (1,)), ((), ())), precision=HIGHEST, preferred_element_type=F32)
        yz[n, z] = out
        send_all(yz.at[n, z], yz.at[n, z], 8, z_peer, n + 2)
        all_landed(yz.at[n], 8, n + 2)
        v = orthonormal(gathered(n))

    place = iota((8, 3 * N), 1)
    mine = z * 32 + pid
    for p in range(3):
        value = jnp.sum(jnp.where(place == p * N + mine, v, 0.0), axis=1, keepdims=True)
        est_ref[:, 0, p : p + 1] = math.sqrt(N) * value[0:3]

    for copy in pending:
        copy.wait_send()


def per_device(polar_rays, first_line, second_line, start_frame):
    first = first_line.reshape(8, 32)
    second = second_line.reshape(8, 32)
    vm = pl.BlockSpec(memory_space=pltpu.VMEM)
    scores, est = pl.pallas_call(
        kernel,
        out_shape=(jax.ShapeDtypeStruct((8, 32), F32), jax.ShapeDtypeStruct((3, 1, 3), F32)),
        in_specs=[
            pl.BlockSpec(memory_space=pl.ANY), vm, vm, pl.BlockSpec(memory_space=pltpu.SMEM), vm,
        ],
        out_specs=(vm, vm),
        scratch_shapes=[
            pltpu.VMEM((8, L, 256), BF16),
            pltpu.VMEM((8, GROUP, 256), BF16),
            pltpu.VMEM((8, 32, 256), BF16),
            pltpu.VMEM((8, 8, 256), F32),
            pltpu.VMEM((8, 8, 256), F32),
            pltpu.VMEM((128, 8), F32),
            pltpu.VMEM((8, 128), F32),
            pltpu.VMEM((8, 128), F32),
            pltpu.VMEM((8, 128), F32),
            pltpu.VMEM((2, 8, 128), F32),
            pltpu.VMEM((32, 8, 128), F32),
            pltpu.VMEM((8, 128), F32),
            pltpu.VMEM((32, 8, 128), F32),
            pltpu.VMEM((ITERS + 1, 8, 8, 128), F32),
            pltpu.VMEM((N, N), BF16),
            pltpu.VMEM((96, 3 * N), F32),
            pltpu.VMEM((128, 3 * N), F32),
            pltpu.SemaphoreType.DMA((48,)),
            pltpu.SemaphoreType.DMA((10,)),
            pltpu.SemaphoreType.DMA((32,)),
            pltpu.SemaphoreType.DMA((2,)),
            pltpu.SemaphoreType.DMA((6,)),
            pltpu.SemaphoreType.DMA((6,)),
        ],
        compiler_params=pltpu.CompilerParams(
            collective_id=0, has_side_effects=True, vmem_limit_bytes=48 << 20
        ),
    )(polar_rays, first, second, second, start_frame.reshape(3, 3))
    return scores.reshape(first_line.shape), est.transpose(0, 2, 1)


def solution(mesh):
    placed = (
        P(("row", "col"), None, None),
        P("row", None, "col"),
        P("row", None, "col"),
        P(None, None, ("row", "col")),
    )
    return jax.shard_map(
        per_device,
        mesh=mesh,
        in_specs=placed,
        out_specs=(P("row", None, "col"), P(None, None, ("row", "col"))),
        check_vma=False,
    )
```

time: 694 us -> 68.8 us (0.10)
  the two profiles are of different devices: /device:TPU:1 before, /device:TPU:8 now
where the time goes in v1:
time: 68.8 us; the launch traced here: 68.7 us
  Pallas kernels  65.2 us (95%)
  local copies, waits for them, and re-layouts  2.78 us (4%)
    pallas_call x1, Pallas kernels, per_device(): pl.pallas_call(kernel, out_shape=(jax.ShapeDtypeStruct((8, 32), F32), jax...  65.2 us
    unnamed x9, local copies, waits for them, and re-layouts  2.78 us

profile of v1, /device:TPU:8, one launch (start us, length us, event | category | flops | bytes accessed | tf_op | source)
XLA Modules:
  0.0 68.7 jit_solution(17955354359456508707)
XLA Ops:
  0.6 0.0 copy-start.2
  0.6 0.0 copy-start.1
  0.7 0.7 %copy.9 = f32[3,3,1]{1,0,2:T(4,128)S(1)} copy(f32[3,3,1]{1,2,0:T(1,128)} %param.7) | data formatting | bytes 72
  1.3 0.0 copy-done.2
  1.3 0.0 copy-done.1
  1.3 0.0 copy-start
  1.4 0.9 %copy-done = bf16[1,360,256]{2,1,0:T(8,128)(2,1)S(1)} copy-done((bf16[1,360,256]{2,1,0:T(8,128)(2,1)S(1)}, bf16[1,360,256]{2,1,0:T(8,128)(2,1)}, u32[]{:S(2)}) %copy-start) | copy-done | bytes 184344
  2.3 65.2 %shard_map.59 = (f32[8,32]{1,0:T(8,128)S(1)}, f32[3,1,3]{2,1,0:T(1,128)S(1)}) custom-call(bf16[1,360,256]{2,1,0:T(8,128)(2,1)S(1)} %copy-done, s32[8,32]{1,0:T(8,128)S(1)} %bitcast.12, s32[8,32]{1,0:T(8,128)S(1)} %bitcast.9, s32[8,32]{1,0:T(8,128)S(1)} %bitcast.10, f32[3,3]{1,0:T(4,128)S(1)} %bitcast.11), custom_call_target="tpu_custom_call" | custom-call | tf_op jit(solution)/shard_map/pallas_call | solution.py:422
  67.5 0.6 copy.12
  68.1 0.6 copy.13
Async XLA Ops:
  0.6 0.7 %copy-start.2 = (s32[8,32,1]{1,2,0:T(1,128)S(1)}, s32[8,32,1]{1,2,0:T(1,128)}, u32[]{:S(2)}) copy-start(s32[8,32,1]{1,2,0:T(1,128)} %param.5) | copy-start | bytes 3076
  0.6 0.7 %copy-start.1 = (s32[8,32,1]{1,2,0:T(1,128)S(1)}, s32[8,32,1]{1,2,0:T(1,128)}, u32[]{:S(2)}) copy-start(s32[8,32,1]{1,2,0:T(1,128)} %param.6) | copy-start | bytes 3076
  1.3 0.9 %copy-start = (bf16[1,360,256]{2,1,0:T(8,128)(2,1)S(1)}, bf16[1,360,256]{2,1,0:T(8,128)(2,1)}, u32[]{:S(2)}) copy-start(bf16[1,360,256]{2,1,0:T(8,128)(2,1)} %rays.1) | copy-start | bytes 552964
